TPU v7x, 128 devices: a whole 4x4x4 slice. The times are simulated.
128 devices in a mesh: gx: 16 (over y, z), gy: 8 (over x, core).
Axes of the slice: x: 4, y: 4, z: 4, core: 2. Of those that a mesh axis runs over, the one named last changes fastest.
Arguments:
- features: bfloat16 [2048, 512, 128], P('gx', 'gy'), may hold values from -6 to 6
- cotangent: bfloat16 [2048, 512, 128], P('gx', 'gy'), may hold values from -31 to 31
- kernel: float32 [7, 7, 128], replicated, may hold values from -0.875 to 0.875
- kernel_bias: float32 [128], replicated, may hold values from -3 to 3
- norm_gain: float32 [128], replicated, may hold values from 0.1 to 1.9
- norm_shift: float32 [128], replicated, may hold values from -3 to 3
- w_up: bfloat16 [128, 512], replicated, may hold values from -0.5 to 0.5
- b_up: float32 [512], replicated, may hold values from -3 to 3
- w_down: bfloat16 [512, 128], replicated, may hold values from -0.25 to 0.25
- b_down: float32 [128], replicated, may hold values from -3 to 3
- layer_scale: float32 [128], replicated, may hold values from 0.3 to 3
Outputs:
- d_features: bfloat16 [2048, 512, 128], P('gx', 'gy')
- d_kernel: float32 [7, 7, 128], replicated
- d_kernel_bias: float32 [128], replicated
- d_norm_gain: float32 [128], replicated
- d_norm_shift: float32 [128], replicated
- d_w_up: float32 [128, 512], replicated
- d_b_up: float32 [512], replicated
- d_w_down: float32 [512, 128], replicated
- d_b_down: float32 [128], replicated
- d_layer_scale: float32 [128], replicated
All inputs are finite; a program needn't handle non-finite values.
Results may differ from a plain program's by a relative error of at most 0.0072.
Values may be sent and summed in bfloat16 or wider, within the bound.
No kernel may reach another device: no remote copies, remote signals or barrier semaphores. Data moves between devices by JAX's collectives and lax.ppermute only.
A program may use at most 64 MiB of HBM per device.

v0:
```python
import math
import jax
import jax.numpy as jnp
from jax import lax
from jax.sharding import PartitionSpec as P

EPSILON = 1e-06


def extended(cells, sides, width):
    for axis, dim in sides:
        count = lax.axis_size(axis)
        head = lax.slice_in_dim(cells, 0, width, axis=dim)
        tail = lax.slice_in_dim(cells, cells.shape[dim] - width, cells.shape[dim], axis=dim)
        cells = jnp.concatenate(
            [
                lax.ppermute(tail, axis, [(i, (i + 1) % count) for i in range(count)]),
                cells,
                lax.ppermute(head, axis, [((i + 1) % count, i) for i in range(count)]),
            ],
            axis=dim,
        )
    return cells


def gelu_pair(hidden):
    erf_part = jax.scipy.special.erf(hidden * 0.7071067811865476)
    value = 0.5 * hidden * (1.0 + erf_part)
    slope_value = (
        0.5 * (1.0 + erf_part) + hidden * jnp.exp(-0.5 * hidden * hidden) * 0.3989422804014327
    )
    return (value, slope_value)


def product(spec, left, right):
    return jnp.einsum(spec, left, right, preferred_element_type=jnp.float32)


def depthwise(padded, kernel, row_count, col_count):
    tap_count = kernel.shape[0]
    accum = jnp.zeros((row_count, col_count, kernel.shape[2]), jnp.float32)
    for row_tap in range(tap_count):
        for col_tap in range(tap_count):
            window = padded[row_tap : row_tap + row_count, col_tap : col_tap + col_count]
            accum = accum + window.astype(jnp.float32) * kernel[row_tap, col_tap]
    return accum


def spread_back(padded, kernel, row_count, col_count):
    tap_count = kernel.shape[0]
    edge_cells = tap_count - 1
    accum = jnp.zeros((row_count, col_count, kernel.shape[2]), jnp.float32)
    for row_tap in range(tap_count):
        for col_tap in range(tap_count):
            window = padded[
                edge_cells - row_tap : edge_cells - row_tap + row_count,
                edge_cells - col_tap : edge_cells - col_tap + col_count,
            ]
            accum = accum + window * kernel[row_tap, col_tap]
    return accum


def kernel_grad(slopes_in, padded, tap_count):
    row_count, col_count = (slopes_in.shape[0], slopes_in.shape[1])
    rows_out = []
    for row_tap in range(tap_count):
        line = []
        for col_tap in range(tap_count):
            window = padded[row_tap : row_tap + row_count, col_tap : col_tap + col_count].astype(
                jnp.float32
            )
            line.append(jnp.sum(slopes_in * window, axis=(0, 1)))
        rows_out.append(jnp.stack(line, 0))
    return jnp.stack(rows_out, 0)


def mask_edges(padded, width):
    col_total = padded.shape[1]
    inner_cols = col_total - 2 * width
    grid_cols = inner_cols * lax.axis_size("gy")
    col_place = lax.axis_index("gy") * inner_cols + lax.iota(jnp.int32, col_total) - width
    keep_mask = (col_place >= 0) & (col_place < grid_cols)
    return jnp.where(keep_mask[None, :, None], padded, jnp.zeros((), padded.dtype))


def layer_back(conv_out, cotan, norm_gain, norm_shift, w_up, b_up, w_down, b_down, layer_scale):
    chan_mean = jnp.mean(conv_out, axis=-1, keepdims=True)
    centred = conv_out - chan_mean
    inv_std = lax.rsqrt(jnp.mean(centred * centred, axis=-1, keepdims=True) + EPSILON)
    normed = centred * inv_std
    normal_out = (normed * norm_gain + norm_shift).astype(jnp.bfloat16)
    hidden = product("rwc,ce->rwe", normal_out, w_up) + b_up
    active, gelu_slope = gelu_pair(hidden)
    active = active.astype(jnp.bfloat16)
    output = product("rwe,ec->rwc", active, w_down) + b_down
    cot_float = cotan.astype(jnp.float32)
    d_output = (cot_float * layer_scale).astype(jnp.bfloat16)
    d_active = product("rwc,ec->rwe", d_output, w_down)
    d_hidden = (d_active * gelu_slope).astype(jnp.bfloat16)
    d_normal = product("rwe,ce->rwc", d_hidden, w_up)
    d_normed = d_normal * norm_gain
    first_mean = jnp.mean(d_normed, axis=-1, keepdims=True)
    second_mean = jnp.mean(d_normed * normed, axis=-1, keepdims=True)
    d_conv = inv_std * (d_normed - first_mean - normed * second_mean)
    d_gain = jnp.sum(d_normal * normed, axis=(0, 1))
    d_shift = jnp.sum(d_normal, axis=(0, 1))
    d_wup = product("rwc,rwe->ce", normal_out, d_hidden)
    d_bup = jnp.sum(d_hidden.astype(jnp.float32), axis=(0, 1))
    d_wdown = product("rwe,rwc->ec", active, d_output)
    d_bdown = jnp.sum(d_output.astype(jnp.float32), axis=(0, 1))
    d_lscale = jnp.sum(cot_float * output, axis=(0, 1))
    return (d_conv, (d_gain, d_shift, d_wup, d_bup, d_wdown, d_bdown, d_lscale))


def local(
    features,
    cotangent,
    kernel,
    kernel_bias,
    norm_gain,
    norm_shift,
    w_up,
    b_up,
    w_down,
    b_down,
    layer_scale,
):
    tap_count = kernel.shape[0]
    reach_cells = tap_count // 2
    row_count, col_count = (features.shape[0], features.shape[1])
    padded_x = mask_edges(extended(features, (("gx", 0), ("gy", 1)), reach_cells), reach_cells)
    conv_out = depthwise(padded_x, kernel, row_count, col_count) + kernel_bias
    d_conv, layer_grads = layer_back(
        conv_out, cotangent, norm_gain, norm_shift, w_up, b_up, w_down, b_down, layer_scale
    )
    d_kern = kernel_grad(d_conv, padded_x, tap_count)
    d_kbias = jnp.sum(d_conv, axis=(0, 1))
    padded_slope = mask_edges(extended(d_conv, (("gx", 0), ("gy", 1)), reach_cells), reach_cells)
    spread = spread_back(padded_slope, kernel, row_count, col_count)
    d_features = (cotangent.astype(jnp.float32) + spread).astype(jnp.bfloat16)
    d_gain, d_shift, d_wup, d_bup, d_wdown, d_bdown, d_lscale = layer_grads
    summed = lax.psum(
        (d_kern, d_kbias, d_gain, d_shift, d_wup, d_bup, d_wdown, d_bdown, d_lscale), ("gx", "gy")
    )
    factor = 1.0 / math.sqrt(row_count * col_count * lax.axis_size("gx") * lax.axis_size("gy"))
    return (d_features,) + tuple((entry * factor for entry in summed))


def solution(mesh):
    placed = (P("gx", "gy", None), P("gx", "gy", None), P(), P(), P(), P(), P(), P(), P(), P(), P())
    return jax.shard_map(
        local,
        mesh=mesh,
        in_specs=placed,
        out_specs=(P("gx", "gy", None), P(), P(), P(), P(), P(), P(), P(), P(), P()),
        check_vma=False,
    )
```

profile of v0, /device:TPU:1, one launch (start us, length us, event | category | flops | bytes accessed | tf_op | source)
XLA Modules:
  0.0 487.0 jit_solution(8291468814353680774)
XLA Ops:
  7.2 0.0 copy-start
  7.2 0.0 copy-start.6
  7.2 0.0 all-reduce.4.cloned.1.call-start
  7.3 0.0 copy-start.3
  7.3 3.1 copy.22
  10.4 0.1 fusion.166
  10.4 2.5 collective-permute-start
  13.0 4.9 %collective-permute-start.1 = (bf16[3,64,128]{2,0,1:T(4,128)(2,1)S(1)}, bf16[3,64,128]{2,0,1:T(4,128)(2,1)S(1)}, u32[]{:S(2)}, u32[]{:S(2)}) collective-permute-start(bf16[3,64,128]{2,0,1:T(4,128)(2,1)S(1)} %get-tuple-element.93), channel_id=1, source_target_pairs={{8,0},{16,8},{24,16},{32,24},{40,32},{48,40},{56,48},{64,56},{72,6... | collective-permute-start | bytes 147464 | tf_op jit(solution)/shard_map/ppermute | solution.py:19
  17.9 0.0 copy-done.6
  18.0 1.1 convert_reduce_fusion.1
  19.1 0.1 collective-permute-done
  19.2 0.1 collective-permute-done.1
  19.2 0.1 pad_maximum_fusion.5
  19.3 2.6 collective-permute-start.2
  21.9 0.0 collective-permute-start.3
  21.9 1.7 collective-permute-done.2
  23.6 2.4 collective-permute-done.3
  26.0 2.9 maximum_select_fusion.1
  29.0 33.0 %fusion.163 = (f32[128,64]{0,1:T(8,128)S(1)}, f32[128,64,128]{2,0,1:T(8,128)S(1)}) fusion(f32[128]{0:T(128)S(1)} %copy-done.11, f32[128]{0:T(128)S(1)} %get-tuple-element.141, bf16[134,70,128]{2,0,1:T(8,128)(2,1)S(1)} %maximum_select_fusion.1, f32[128]{0:T(128)S(1)} %get-tuple-element.142, f32[128]{0:T(128)S(1)} %get-tuple-element.95, ...), kind=kLoop, calls=%fused_computation.403 | loop fusion | flops 155181056 | bytes 107013120 | tf_op jit(solution)/shard_map/reduce_sum | solution.py:87
  62.0 0.0 copy-start.7
  62.0 0.0 copy-start.8
  62.0 0.0 copy-start.9
  62.0 2.7 multiply_reduce_fusion.2
  64.8 0.0 copy-start.4
  64.8 0.0 copy-start.12
  64.8 8.6 %multiply_convert_fusion = (bf16[128,64,512]{2,0,1:T(8,128)(2,1)}, f32[128,64,512]{2,0,1:T(8,128)S(1)}) fusion(f32[512]{0:T(512)S(1)} %copy-done.9, bf16[128,512]{1,0:T(8,128)(2,1)S(1)} %copy-done, f32[128,64,128]{2,0,1:T(8,128)S(1)} %get-tuple-element.85, f32[128]{0:T(128)S(1)} %copy-done.8, f32[128]{0:T(128)S(1)} %copy-done.7, ...), kind=kOutput, calls=%fused_computation.7 | convolution fusion | flops 1104150528 | bytes 29559808 | tf_op jit(solution)/shard_map/rwc,ce->rwe/dot_general | solution.py:36
  73.5 10.9 %convert_reduce_fusion = (f32[512]{0:T(512)S(1)}, bf16[128,64,512]{2,0,1:T(8,128)(2,1)S(1)}) fusion(f32[128,64,512]{2,0,1:T(8,128)S(1)} %get-tuple-element.147, f32[512]{0:T(512)S(1)} %copy-done.9, bf16[512,128]{1,0:T(8,128)(2,1)S(1)} %copy-done.12, f32[128]{0:T(128)S(1)} %copy-done.10, bf16[128,64,128]{2,1,0:T(8,128)(2,1)S(1)} %copy-done.4), kind=kOutput, calls=%fused_computation.8 | convolution fusion | flops 1131412992 | bytes 27398656 | tf_op jit(solution)/shard_map/rwc,ec->rwe/dot_general | solution.py:36
  84.4 4.2 convolution_bitcast_fusion.1
  88.6 4.8 multiply_reduce_fusion
  93.3 0.0 slice-start
  93.3 13.4 %fusion.102 = (f32[128]{0:T(128)S(1)}, f32[128]{0:T(128)S(1)}, f32[128]{0:T(128)S(1)}, f32[128]{0:T(128)S(1)}, f32[128]{0:T(128)S(1)}, /*index=5*/f32[128]{0:T(1...) fusion(bf16[134,70,128]{2,0,1:T(8,128)(2,1)S(1)} %maximum_selec, ...), kind=kLoop, calls=%fused_computation.208 | loop fusion | flops 63960832 | bytes 50472448 | tf_op jit(solution)/shard_map/reduce_sum | solution.py:72
  106.7 0.0 copy-start.2
  106.8 0.0 slice-start.1
  106.8 11.0 %fusion.84 = (f32[128]{0:T(128)S(1)}, f32[128]{0:T(128)S(1)}, f32[128]{0:T(128)S(1)}, f32[128]{0:T(128)S(1)}, f32[128]{0:T(128)S(1)}, /*index=5*/f32[128]{0:T(12...) fusion(f32[128,64,128]{2,0,1:T(8,128)S(1)} %get-tuple-element.8, ...), kind=kLoop, calls=%fused_computation.190 | loop fusion | flops 56620800 | bytes 41952256 | tf_op jit(solution)/shard_map/reduce_sum | solution.py:72
  117.8 0.0 copy-start.5
  117.8 8.2 %fusion.43 = (f32[128]{0:T(128)S(1)}, f32[128]{0:T(128)S(1)}, f32[128]{0:T(128)S(1)}, f32[128]{0:T(128)S(1)}, f32[128]{0:T(128)S(1)}, /*index=5*/f32[128]{0:T(12...) fusion(f32[128,64,128]{2,0,1:T(8,128)S(1)} %get-tuple-element.8, ...), kind=kLoop, calls=%fused_computation.149 | loop fusion | flops 41941248 | bytes 31464448 | tf_op jit(solution)/shard_map/reduce_sum | solution.py:72
  126.2 0.0 copy-start.13
  126.2 4.3 convolution_bitcast_fusion
  130.5 0.0 copy-done.13
  130.5 6.2 %fusion.105 = f32[128]{0:T(128)S(1)} fusion(bf16[128,64,512]{2,0,1:T(8,128)(2,1)} %get-tuple-element.146, f32[128]{0:T(128)S(1)} %copy-done.13, bf16[128,64,128]{2,1,0:T(8,128)(2,1)S(1)} %copy-done.5, bf16[512,128]{1,0:T(8,128)(2,1)S(1)} %copy-done.12), kind=kOutput, calls=%fused_computation.211 | convolution fusion | flops 1077936000 | bytes 10617856 | tf_op jit(solution)/shard_map/rwe,ec->rwc/dot_general | solution.py:36
  137.0 67.9 %all-reduce = (f32[7,7,128]{2,1,0:T(8,128)S(1)}, f32[128]{0:T(128)S(1)}, f32[128]{0:T(128)S(1)}, f32[128]{0:T(128)S(1)}, f32[512]{0:T(512)S(1)}, /*index=5*/f32[128]{0:T(128)S(1)}, f32[128]{0:T(128)S(1)}) all-reduce(f32[7,7,128]{2,1,0:T(8,128)S(1)} %constant_dynamic-update-slice_fusion, ...), channel_id=1, replica_groups=mesh['gx'=16,'gy'=8] {'gx','gy'}, use_global_device_ids=true, to_apply=%region_53.54 | all-reduce | flops 7424 | bytes 59392 | tf_op jit(solution)/shard_map/psum | solution.py:142
  204.9 0.6 broadcast_multiply_fusion.5
  205.6 0.6 broadcast_multiply_fusion.6
  206.1 0.5 broadcast_multiply_fusion.10
  206.6 0.5 broadcast_multiply_fusion.11
  207.2 0.5 broadcast_multiply_fusion.7
  207.7 0.5 broadcast_multiply_fusion.8
  208.2 0.0 collective-permute-start.4
  208.2 4.8 collective-permute-start.5
  213.0 0.0 all-reduce.4.cloned.1.call-update
  213.0 0.5 broadcast_multiply_fusion.9
  213.5 1.8 collective-permute-done.4
  215.3 0.0 collective-permute-done.5
  215.3 1.1 pad_maximum_fusion.2
  216.4 1.5 collective-permute-start.6
  217.9 0.8 collective-permute-start.7
  218.8 136.7 %all-reduce.4.cloned.1.call-done = (f32[128,512]{1,0:T(8,128)}, f32[512,128]{1,0:T(8,128)}) async-done(((f32[128,512]{1,0:T(8,128)}, f32[512,128]{1,0:T(8,128)}), (f32[128,512]{1,0:T(8,128)}, f32[512,128]{1,0:T(8,128)})) %all-reduce.4.cloned.1.call-update) | async-done | bytes 524304 | tf_op jit(solution)/shard_map/psum | solution.py:142
  355.4 1.7 broadcast_multiply_fusion
  357.1 1.7 broadcast_multiply_fusion.1
  358.8 0.0 collective-permute-done.6
  358.8 0.0 collective-permute-done.7
  358.8 5.5 %maximum_select_fusion = f32[134,70,128]{2,0,1:T(8,128)} fusion(f32[134,3,128]{2,0,1:T(8,128)S(1)} %collective-permute-done.7, f32[3,64,128]{2,0,1:T(4,128)S(1)} %collective-permute-done.5, f32[128,64,128]{2,0,1:T(8,128)} %copy-done.2, f32[3,64,128]{2,0,1:T(4,128)S(1)} %collective-permute-done.4, f32[134,3,128]{2,0,1:T(8,128)S(1)} %collective-permute-done.6, ...), kind=kLoop, calls=%fused_computation.111 | loop fusion | flops 6003200 | bytes 9605190 | tf_op jit(solution)/shard_map/jit(_where)/select_n | solution.py:83
  364.3 111.4 %fusion.104 = bf16[128,64,128]{2,0,1:T(8,128)(2,1)} fusion(f32[134,70,128]{2,0,1:T(8,128)} %maximum_select_fusion, f32[128]{0:T(128)S(1)} %get-tuple-element.141, f32[128]{0:T(128)S(1)} %get-tuple-element.142, f32[128]{0:T(128)S(1)} %get-tuple-element.95, f32[128]{0:T(128)S(1)} %get-tuple-element.96, f32[128]{0:T(128)S(1)} %get-tuple-element.97, ...), kind=kLoop, calls=%fused_computation.210 | loop fusion | flops 104857600 | bytes 209740288 | tf_op jit(solution)/shard_map/convert_element_type | solution.py:140
  475.7 4.3 copy.27
  (40 shorter events, 0.4 us)
Async XLA Ops:
  7.2 57.6 %copy-start = (bf16[128,512]{1,0:T(8,128)(2,1)S(1)}, bf16[128,512]{1,0:T(8,128)(2,1)}, u32[]{:S(2)}) copy-start(bf16[128,512]{1,0:T(8,128)(2,1)} %param.17) | copy-start | bytes 393220
  7.2 10.7 %copy-start.6 = (f32[7,7,128]{2,1,0:T(8,128)S(1)}, f32[7,7,128]{2,1,0:T(8,128)}, u32[]{:S(2)}) copy-start(f32[7,7,128]{2,1,0:T(8,128)} %param.13) | copy-start | bytes 75268
  7.2 10.7 %copy-start.10 = (f32[128]{0:T(128)S(1)}, f32[128]{0:T(128)}, u32[]{:S(2)}) copy-start(f32[128]{0:T(128)} %param.21) | copy-start | bytes 1540
  7.2 348.2 %all-reduce.4.cloned.1.call-start = ((), (), s32[]{:S(2)}) async-start(), calls=%async_computation | async-start | bytes 1048576 | tf_op jit(solution)/shard_map/psum | solution.py:142
  7.3 10.7 %copy-start.3 = (bf16[128,64,128]{2,1,0:T(8,128)(2,1)S(1)}, bf16[128,64,128]{2,1,0:T(8,128)(2,1)}, u32[]{:S(2)}) copy-start(bf16[128,64,128]{2,1,0:T(8,128)(2,1)} %param.12) | copy-start | bytes 6291460
  10.4 8.8 %collective-permute-start = (bf16[3,64,128]{2,0,1:T(4,128)(2,1)S(1)}, bf16[3,64,128]{2,0,1:T(4,128)(2,1)S(1)}, u32[]{:S(2)}, u32[]{:S(2)}) collective-permute-start(bf16[3,64,128]{2,0,1:T(4,128)(2,1)S(1)} %get-tuple-element.92), channel_id=1, source_target_pairs={{0,8},{8,16},{16,24},{24,32},{32,40},{40,48},{48,56},{56,64},{64,7... | collective-permute-start | bytes 147464 | tf_op jit(solution)/shard_map/ppermute | solution.py:17
  13.0 6.3 %collective-permute-start.1 = (bf16[3,64,128]{2,0,1:T(4,128)(2,1)S(1)}, bf16[3,64,128]{2,0,1:T(4,128)(2,1)S(1)}, u32[]{:S(2)}, u32[]{:S(2)}) collective-permute-start(bf16[3,64,128]{2,0,1:T(4,128)(2,1)S(1)} %get-tuple-element.93), channel_id=1, source_target_pairs={{8,0},{16,8},{24,16},{32,24},{40,32},{48,40},{56,48},{64,56},{72,6... | collective-permute-start | bytes 147464 | tf_op jit(solution)/shard_map/ppermute | solution.py:19
  19.1 9.9 %copy-start.11 = (f32[128]{0:T(128)S(1)}, f32[128]{0:T(128)}, u32[]{:S(2)}) copy-start(f32[128]{0:T(128)} %param.14) | copy-start | bytes 1540
  19.3 4.3 collective-permute-start.2
  21.9 4.1 collective-permute-start.3
  62.0 2.8 copy-start.7
  62.0 2.8 copy-start.8
  62.0 2.8 copy-start.9
  64.8 8.7 %copy-start.4 = (bf16[128,64,128]{2,1,0:T(8,128)(2,1)S(1)}, bf16[128,64,128]{2,1,0:T(8,128)(2,1)}, u32[]{:S(2)}) copy-start(bf16[128,64,128]{2,1,0:T(8,128)(2,1)} %param.12) | copy-start | bytes 6291460
  64.8 8.6 %copy-start.12 = (bf16[512,128]{1,0:T(8,128)(2,1)S(1)}, bf16[512,128]{1,0:T(8,128)(2,1)}, u32[]{:S(2)}) copy-start(bf16[512,128]{1,0:T(8,128)(2,1)} %param.19) | copy-start | bytes 393220
  93.3 32.8 %slice-start = ((s8[8388608]{0:T(1024)(128)(4,1)}), s8[4194304]{0:T(1024)(128)(4,1)S(1)}, s32[]{:S(2)}) async-start(s8[8388608]{0:T(1024)(128)(4,1)} %bitcast.185), calls=%async_computation.1 | async-start | bytes 8388608
  106.7 19.3 %copy-start.2 = (f32[128,64,128]{2,0,1:T(8,128)}, f32[128,64,128]{2,0,1:T(8,128)S(1)}, u32[]{:S(2)}) copy-start(f32[128,64,128]{2,0,1:T(8,128)S(1)} %get-tuple-element.83) | copy-start | bytes 12582916
  106.8 19.4 %slice-start.1 = ((s8[8388608]{0:T(1024)(128)(4,1)}), s8[4194304]{0:T(1024)(128)(4,1)S(1)}, s32[]{:S(2)}) async-start(s8[8388608]{0:T(1024)(128)(4,1)} %bitcast.185), calls=%async_computation.2 | async-start | bytes 8388608
  117.8 8.3 %copy-start.5 = (bf16[128,64,128]{2,1,0:T(8,128)(2,1)S(1)}, bf16[128,64,128]{2,1,0:T(8,128)(2,1)}, u32[]{:S(2)}) copy-start(bf16[128,64,128]{2,1,0:T(8,128)(2,1)} %param.12) | copy-start | bytes 6291460
  126.2 4.4 copy-start.13
  208.2 7.1 %collective-permute-start.4 = (f32[3,64,128]{2,0,1:T(4,128)S(1)}, f32[3,64,128]{2,0,1:T(4,128)S(1)}, u32[]{:S(2)}, u32[]{:S(2)}) collective-permute-start(f32[3,64,128]{2,0,1:T(4,128)S(1)} %get-tuple-element.88), channel_id=1, source_target_pairs={{0,8},{8,16},{16,24},{24,32},{32,40},{40,48},{48,56},{56,64},{64,7... | collective-permute-start | bytes 294920 | tf_op jit(solution)/shard_map/ppermute | solution.py:17
  208.2 7.1 %collective-permute-start.5 = (f32[3,64,128]{2,0,1:T(4,128)S(1)}, f32[3,64,128]{2,0,1:T(4,128)S(1)}, u32[]{:S(2)}, u32[]{:S(2)}) collective-permute-start(f32[3,64,128]{2,0,1:T(4,128)S(1)} %get-tuple-element.89), channel_id=1, source_target_pairs={{8,0},{16,8},{24,16},{32,24},{40,32},{48,40},{56,48},{64,56},{72,6... | collective-permute-start | bytes 294920 | tf_op jit(solution)/shard_map/ppermute | solution.py:19
  216.4 142.4 %collective-permute-start.6 = (f32[134,3,128]{2,0,1:T(8,128)S(1)}, f32[134,3,128]{2,0,1:T(8,128)S(1)}, u32[]{:S(2)}, u32[]{:S(2)}) collective-permute-start(f32[134,3,128]{2,0,1:T(8,128)S(1)} %get-tuple-element.86), channel_id=1, source_target_pairs={{0,1},{1,2},{2,3},{3,4},{4,5},{5,6},{6,7},{7,0},{8,9},{9,10},{10,1... | collective-permute-start | bytes 617480 | tf_op jit(solution)/shard_map/ppermute | solution.py:17
  217.9 140.9 %collective-permute-start.7 = (f32[134,3,128]{2,0,1:T(8,128)S(1)}, f32[134,3,128]{2,0,1:T(8,128)S(1)}, u32[]{:S(2)}, u32[]{:S(2)}) collective-permute-start(f32[134,3,128]{2,0,1:T(8,128)S(1)} %get-tuple-element.87), channel_id=1, source_target_pairs={{1,0},{2,1},{3,2},{4,3},{5,4},{6,5},{7,6},{0,7},{9,8},{10,9},{11,1... | collective-permute-start | bytes 617480 | tf_op jit(solution)/shard_map/ppermute | solution.py:19
  364.3 115.7 %copy-start.1 = (bf16[128,512]{1,0:T(8,128)(2,1)S(1)}, bf16[128,512]{1,0:T(8,128)(2,1)}, u32[]{:S(2)}) copy-start(bf16[128,512]{1,0:T(8,128)(2,1)} %param.17) | copy-start | bytes 393220
Sparse Core Ops, SparseCore 0:
  213.1 142.2 all-reduce.3
where the time goes:
time: 490 us; the launch traced here: 487 us
  other arithmetic  198 us (40%)
  waiting for transfers between devices  143 us (29%)
  blocking collectives  67.9 us (14%)
  matrix products  39 us (8%)
  starting transfers between devices  17.3 us (4%)
  between operations  14.7 us (3%)
  local copies, waits for them, and re-layouts  7.79 us (2%)
    psum x1, waiting for transfers between devices, local(): lax.psum((d_kern, d_kbias, d_gain, d_shift, d_wup, d_bup, d_wdown, d_bdow...  137 us
    convert_element_type x1, other arithmetic, local(): d_features = (cotangent.astype(jnp.float32) + spread).astype(jnp.bfloat16)  111 us
    psum x1, blocking collectives, local(): lax.psum((d_kern, d_kbias, d_gain, d_shift, d_wup, d_bup, d_wdown, d_bdow...  67.9 us
    dot_general x6, matrix products, product(): return jnp.einsum(spec, left, right, preferred_element_type=jnp.float32)  39 us
    reduce_sum x1, other arithmetic, layer_back(): chan_mean = jnp.mean(conv_out, axis=-1, keepdims=True)  33 us
    reduce_sum x3, other arithmetic, kernel_grad(): line.append(jnp.sum(slopes_in * window, axis=(0, 1)))  32.6 us
    ppermute x4, starting transfers between devices, extended(): lax.ppermute(head, axis, [((i + 1) % count, i) for i in range(count)])  10.6 us
  transfers between devices with their start and end apart: 9, of which 5 were waited for; matrix products, arithmetic and copies ran while one was open for 1% of the time, Pallas kernels for 0%

commit v1 on v0

--- a/solution.py
+++ b/solution.py
@@ -140,7 +140,10 @@
     d_features = (cotangent.astype(jnp.float32) + spread).astype(jnp.bfloat16)
     d_gain, d_shift, d_wup, d_bup, d_wdown, d_bdown, d_lscale = layer_grads
     summed = lax.psum(
-        (d_kern, d_kbias, d_gain, d_shift, d_wup, d_bup, d_wdown, d_bdown, d_lscale), ("gx", "gy")
+        lax.psum(
+            (d_kern, d_kbias, d_gain, d_shift, d_wup, d_bup, d_wdown, d_bdown, d_lscale), "gx"
+        ),
+        "gy",
     )
     factor = 1.0 / math.sqrt(row_count * col_count * lax.axis_size("gx") * lax.axis_size("gy"))
     return (d_features,) + tuple((entry * factor for entry in summed))

time: 490 us -> 452 us (0.922)
  waiting for transfers between devices: 143 us -> 75.3 us
  blocking collectives: 67.9 us -> 96.1 us
    psum x1, waiting for transfers between devices: 137 us -> 66.7 us  [local(): lax.psum((d_kern, d_kbias, d_gain, d_shift, d_wup, d_bup, d_wdown, d_bdow...]
    psum x0 -> x1, blocking collectives: none -> 34.9 us  [local(): lax.psum(lax.psum((d_kern, d_kbias, d_gain, d_shift, d_wup, d_bup, d_wdow...]
    psum x1, blocking collectives: 67.9 us -> 61.2 us  [local(): lax.psum((d_kern, d_kbias, d_gain, d_shift, d_wup, d_bup, d_wdown, d_bdow...]
  transfers between devices with their start and end apart: 9 -> 10, of which waited for: 5 -> 7; matrix products, arithmetic and copies ran while one was open for 1% -> 27% of each run, Pallas kernels for 0% -> 0%
where the time goes in v1:
time: 452 us; the launch traced here: 449 us
  other arithmetic  196 us (43%)
  blocking collectives  96.1 us (21%)
  waiting for transfers between devices  75.3 us (17%)
  matrix products  39 us (9%)
  starting transfers between devices  19.5 us (4%)
  between operations  14.7 us (3%)
  local copies, waits for them, and re-layouts  7.8 us (2%)
    convert_element_type x1, other arithmetic, local(): d_features = (cotangent.astype(jnp.float32) + spread).astype(jnp.bfloat16)  112 us
    psum x1, waiting for transfers between devices, local(): lax.psum((d_kern, d_kbias, d_gain, d_shift, d_wup, d_bup, d_wdown, d_bdow...  66.7 us
    psum x1, blocking collectives, local(): lax.psum((d_kern, d_kbias, d_gain, d_shift, d_wup, d_bup, d_wdown, d_bdow...  61.2 us
    dot_general x6, matrix products, product(): return jnp.einsum(spec, left, right, preferred_element_type=jnp.float32)  39 us
    psum x1, blocking collectives, local(): lax.psum(lax.psum((d_kern, d_kbias, d_gain, d_shift, d_wup, d_bup, d_wdow...  34.9 us
    reduce_sum x1, other arithmetic, layer_back(): chan_mean = jnp.mean(conv_out, axis=-1, keepdims=True)  33.1 us
    reduce_sum x3, other arithmetic, kernel_grad(): line.append(jnp.sum(slopes_in * window, axis=(0, 1)))  32.6 us
    ppermute x4, starting transfers between devices, extended(): lax.ppermute(head, axis, [((i + 1) % count, i) for i in range(count)])  11.9 us
  transfers between devices with their start and end apart: 10, of which 7 were waited for; matrix products, arithmetic and copies ran while one was open for 27% of the time, Pallas kernels for 0%

profile of v1, /device:TPU:1, one launch (start us, length us, event | category | flops | bytes accessed | tf_op | source)
XLA Modules:
  0.0 448.6 jit_solution(10525759509758602689)
XLA Ops:
  7.2 0.0 copy-start
  7.2 0.0 all-reduce.7.cloned.1.call-start
  7.3 0.0 copy-start.4
  7.3 3.1 copy.22
  10.4 0.1 fusion.166
  10.4 2.5 collective-permute-start
  13.0 4.9 %collective-permute-start.1 = (bf16[3,64,128]{2,0,1:T(4,128)(2,1)S(1)}, bf16[3,64,128]{2,0,1:T(4,128)(2,1)S(1)}, u32[]{:S(2)}, u32[]{:S(2)}) collective-permute-start(bf16[3,64,128]{2,0,1:T(4,128)(2,1)S(1)} %get-tuple-element.102), channel_id=1, source_target_pairs={{8,0},{16,8},{24,16},{32,24},{40,32},{48,40},{56,48},{64,56},{72,6... | collective-permute-start | bytes 147464 | tf_op jit(solution)/shard_map/ppermute | solution.py:19
  18.0 1.1 convert_reduce_fusion.1
  19.1 0.1 collective-permute-done
  19.2 0.1 collective-permute-done.1
  19.2 0.1 pad_maximum_fusion.5
  19.3 2.6 collective-permute-start.2
  21.9 0.0 collective-permute-start.3
  21.9 1.7 collective-permute-done.2
  23.6 2.4 collective-permute-done.3
  26.0 2.9 maximum_select_fusion.1
  29.0 33.1 %fusion.163 = (f32[128,64]{0,1:T(8,128)S(1)}, f32[128,64,128]{2,0,1:T(8,128)S(1)}) fusion(f32[128]{0:T(128)S(1)} %copy-done.12, f32[128]{0:T(128)S(1)} %get-tuple-element.150, bf16[134,70,128]{2,0,1:T(8,128)(2,1)S(1)} %maximum_select_fusion.1, f32[128]{0:T(128)S(1)} %get-tuple-element.151, f32[128]{0:T(128)S(1)} %get-tuple-element.104, ...), kind=kLoop, calls=%fused_computation.403 | loop fusion | flops 155181056 | bytes 107013120 | tf_op jit(solution)/shard_map/reduce_sum | solution.py:87
  62.1 0.0 copy-start.8
  62.1 0.0 copy-start.9
  62.1 0.0 copy-start.10
  62.1 2.7 multiply_reduce_fusion.2
  64.9 0.0 copy-start.5
  64.9 0.0 copy-start.13
  64.9 8.6 %multiply_convert_fusion = (bf16[128,64,512]{2,0,1:T(8,128)(2,1)}, f32[128,64,512]{2,0,1:T(8,128)S(1)}) fusion(f32[512]{0:T(512)S(1)} %copy-done.10, bf16[128,512]{1,0:T(8,128)(2,1)S(1)} %copy-done, f32[128,64,128]{2,0,1:T(8,128)S(1)} %get-tuple-element.94, f32[128]{0:T(128)S(1)} %copy-done.9, f32[128]{0:T(128)S(1)} %copy-done.8, ...), kind=kOutput, calls=%fused_computation.7 | convolution fusion | flops 1104150528 | bytes 29559808 | tf_op jit(solution)/shard_map/rwc,ce->rwe/dot_general | solution.py:36
  73.6 10.9 %convert_reduce_fusion = (f32[512]{0:T(512)S(1)}, bf16[128,64,512]{2,0,1:T(8,128)(2,1)S(1)}) fusion(f32[128,64,512]{2,0,1:T(8,128)S(1)} %get-tuple-element.156, f32[512]{0:T(512)S(1)} %copy-done.10, bf16[512,128]{1,0:T(8,128)(2,1)S(1)} %copy-done.13, f32[128]{0:T(128)S(1)} %copy-done.11, bf16[128,64,128]{2,1,0:T(8,128)(2,1)S(1)} %copy-done.5), kind=kOutput, calls=%fused_computation.8 | convolution fusion | flops 1131412992 | bytes 27398656 | tf_op jit(solution)/shard_map/rwc,ec->rwe/dot_general | solution.py:36
  84.5 4.2 convolution_bitcast_fusion.1
  88.6 4.8 %multiply_reduce_fusion = (f32[128]{0:T(128)S(1)}, f32[128,64]{0,1:T(8,128)S(1)}, f32[128,64]{0,1:T(8,128)S(1)}, f32[128]{0:T(128)S(1)}, f32[128,64,128]{2,0,1:T(8,128)S(1)}) fusion(f32[128,64,128]{2,0,1:T(8,128)S(1)} %get-tuple-element.94, f32[128,64]{0,1:T(8,128)S(1)} %add_rsqrt_fusion, f32[128,64]{0,1:T(8,128)S(1)} %broadcast_multiply_fusion.4, ...), kind=kOutput, calls=%fused_computation.310 | convolution fusion | flops 1083162368 | bytes 17040896 | tf_op jit(solution)/shard_map/rwe,ce->rwc/dot_general | solution.py:36
  93.4 0.0 slice-start
  93.4 13.4 %fusion.102 = (f32[128]{0:T(128)S(1)}, f32[128]{0:T(128)S(1)}, f32[128]{0:T(128)S(1)}, f32[128]{0:T(128)S(1)}, f32[128]{0:T(128)S(1)}, /*index=5*/f32[128]{0:T(1...) fusion(bf16[134,70,128]{2,0,1:T(8,128)(2,1)S(1)} %maximum_selec, ...), kind=kLoop, calls=%fused_computation.208 | loop fusion | flops 63960832 | bytes 50472448 | tf_op jit(solution)/shard_map/reduce_sum | solution.py:72
  106.8 0.0 slice-start.1
  106.8 11.0 %fusion.84 = (f32[128]{0:T(128)S(1)}, f32[128]{0:T(128)S(1)}, f32[128]{0:T(128)S(1)}, f32[128]{0:T(128)S(1)}, f32[128]{0:T(128)S(1)}, /*index=5*/f32[128]{0:T(12...) fusion(f32[128,64,128]{2,0,1:T(8,128)S(1)} %get-tuple-element.9, ...), kind=kLoop, calls=%fused_computation.190 | loop fusion | flops 56620800 | bytes 41952256 | tf_op jit(solution)/shard_map/reduce_sum | solution.py:72
  117.9 0.0 copy-start.6
  117.9 8.2 %fusion.43 = (f32[128]{0:T(128)S(1)}, f32[128]{0:T(128)S(1)}, f32[128]{0:T(128)S(1)}, f32[128]{0:T(128)S(1)}, f32[128]{0:T(128)S(1)}, /*index=5*/f32[128]{0:T(12...) fusion(f32[128,64,128]{2,0,1:T(8,128)S(1)} %get-tuple-element.9, ...), kind=kLoop, calls=%fused_computation.149 | loop fusion | flops 41941248 | bytes 31464448 | tf_op jit(solution)/shard_map/reduce_sum | solution.py:72
  126.2 0.0 copy-start.14
  126.2 4.3 convolution_bitcast_fusion
  130.6 6.2 %fusion.105 = f32[128]{0:T(128)S(1)} fusion(bf16[128,64,512]{2,0,1:T(8,128)(2,1)} %get-tuple-element.155, f32[128]{0:T(128)S(1)} %copy-done.14, bf16[128,64,128]{2,1,0:T(8,128)(2,1)S(1)} %copy-done.6, bf16[512,128]{1,0:T(8,128)(2,1)S(1)} %copy-done.13), kind=kOutput, calls=%fused_computation.211 | convolution fusion | flops 1077936000 | bytes 10617856 | tf_op jit(solution)/shard_map/rwe,ec->rwc/dot_general | solution.py:36
  137.1 61.2 %all-reduce = (f32[7,7,128]{2,1,0:T(8,128)S(1)}, f32[128]{0:T(128)S(1)}, f32[128]{0:T(128)S(1)}, f32[128]{0:T(128)S(1)}, f32[512]{0:T(512)S(1)}, /*index=5*/f32[128]{0:T(128)S(1)}, f32[128]{0:T(128)S(1)}) all-reduce(f32[7,7,128]{2,1,0:T(8,128)S(1)} %constant_dynamic-update-slice_fusion, ...), channel_id=1, replica_groups=mesh['gx'=16,'gy'=8] {'gx'}, use_global_device_ids=true, to_apply=%region_53.54 | all-reduce | flops 7424 | bytes 59392 | tf_op jit(solution)/shard_map/psum | solution.py:143
  198.2 34.9 %all-reduce.2 = (f32[7,7,128]{2,1,0:T(8,128)S(1)}, f32[128]{0:T(128)S(1)}, f32[128]{0:T(128)S(1)}, f32[128]{0:T(128)S(1)}, f32[512]{0:T(512)S(1)}, /*index=5*/f32[128]{0:T(128)S(1)}, f32[128]{0:T(128)S(1)}) all-reduce(f32[7,7,128]{2,1,0:T(8,128)S(1)} %get-tuple-element.74, ...), channel_id=1, replica_groups=mesh['gx'=16,'gy'=8] {'gy'}, use_global_device_ids=true, to_apply=%region_54.55 | all-reduce | flops 7424 | bytes 59392 | tf_op jit(solution)/shard_map/psum | solution.py:142
  233.2 0.6 broadcast_multiply_fusion.5
  233.8 0.6 broadcast_multiply_fusion.6
  234.4 0.5 broadcast_multiply_fusion.10
  234.9 0.5 broadcast_multiply_fusion.11
  235.4 0.5 broadcast_multiply_fusion.7
  235.9 0.0 collective-permute-start.4
  235.9 4.8 %collective-permute-start.5 = (f32[3,64,128]{2,0,1:T(4,128)S(1)}, f32[3,64,128]{2,0,1:T(4,128)S(1)}, u32[]{:S(2)}, u32[]{:S(2)}) collective-permute-start(f32[3,64,128]{2,0,1:T(4,128)S(1)} %get-tuple-element.98), channel_id=1, source_target_pairs={{8,0},{16,8},{24,16},{32,24},{40,32},{48,40},{56,48},{64,56},{72,6... | collective-permute-start | bytes 294920 | tf_op jit(solution)/shard_map/ppermute | solution.py:19
  240.7 0.5 broadcast_multiply_fusion.8
  241.2 0.0 all-reduce.7.cloned.1.call-update
  241.2 0.0 all-reduce.9.cloned.1.call-start
  241.3 1.8 collective-permute-done.4
  243.0 0.0 collective-permute-done.5
  243.0 1.1 pad_maximum_fusion.2
  244.1 2.4 collective-permute-start.6
  246.5 2.1 collective-permute-start.7
  248.7 0.5 broadcast_multiply_fusion.9
  249.2 0.4 collective-permute-done.6
  249.6 2.1 collective-permute-done.7
  251.7 3.8 maximum_select_fusion
  255.6 66.7 %all-reduce.7.cloned.1.call-done = (f32[128,512]{1,0:T(8,128)}, f32[512,128]{1,0:T(8,128)}) async-done(((f32[128,512]{1,0:T(8,128)}, f32[512,128]{1,0:T(8,128)}), (f32[128,512]{1,0:T(8,128)}, f32[512,128]{1,0:T(8,128)})) %all-reduce.7.cloned.1.call-update) | async-done | bytes 524304 | tf_op jit(solution)/shard_map/psum | solution.py:143
  322.2 0.0 all-reduce.9.cloned.1.call-update
  322.3 0.0 copy-start.1
  322.3 111.6 %fusion.104 = bf16[128,64,128]{2,0,1:T(8,128)(2,1)} fusion(f32[134,70,128]{2,0,1:T(8,128)} %maximum_select_fusion, f32[128]{0:T(128)S(1)} %get-tuple-element.150, f32[128]{0:T(128)S(1)} %get-tuple-element.151, f32[128]{0:T(128)S(1)} %get-tuple-element.104, f32[128]{0:T(128)S(1)} %get-tuple-element.105, f32[128]{0:T(128)S(1)} %get-tuple-element.106, ...), kind=kLoop, calls=%fused_computation.210 | loop fusion | flops 104857600 | bytes 209740288 | tf_op jit(solution)/shard_map/convert_element_type | solution.py:140
  433.9 4.3 copy.27
  438.2 1.7 broadcast_multiply_fusion
  439.9 1.7 broadcast_multiply_fusion.1
  (46 shorter events, 0.4 us)
Async XLA Ops:
  7.2 57.7 %copy-start = (bf16[128,512]{1,0:T(8,128)(2,1)S(1)}, bf16[128,512]{1,0:T(8,128)(2,1)}, u32[]{:S(2)}) copy-start(bf16[128,512]{1,0:T(8,128)(2,1)} %param.17) | copy-start | bytes 393220
  7.2 10.7 %copy-start.7 = (f32[7,7,128]{2,1,0:T(8,128)S(1)}, f32[7,7,128]{2,1,0:T(8,128)}, u32[]{:S(2)}) copy-start(f32[7,7,128]{2,1,0:T(8,128)} %param.13) | copy-start | bytes 75268
  7.2 10.7 %copy-start.11 = (f32[128]{0:T(128)S(1)}, f32[128]{0:T(128)}, u32[]{:S(2)}) copy-start(f32[128]{0:T(128)} %param.21) | copy-start | bytes 1540
  7.2 315.0 %all-reduce.7.cloned.1.call-start = ((), (), s32[]{:S(2)}) async-start(), calls=%async_computation | async-start | bytes 1048576 | tf_op jit(solution)/shard_map/psum | solution.py:143
  7.3 10.7 %copy-start.4 = (bf16[128,64,128]{2,1,0:T(8,128)(2,1)S(1)}, bf16[128,64,128]{2,1,0:T(8,128)(2,1)}, u32[]{:S(2)}) copy-start(bf16[128,64,128]{2,1,0:T(8,128)(2,1)} %param.12) | copy-start | bytes 6291460
  10.4 8.8 %collective-permute-start = (bf16[3,64,128]{2,0,1:T(4,128)(2,1)S(1)}, bf16[3,64,128]{2,0,1:T(4,128)(2,1)S(1)}, u32[]{:S(2)}, u32[]{:S(2)}) collective-permute-start(bf16[3,64,128]{2,0,1:T(4,128)(2,1)S(1)} %get-tuple-element.101), channel_id=1, source_target_pairs={{0,8},{8,16},{16,24},{24,32},{32,40},{40,48},{48,56},{56,64},{64,7... | collective-permute-start | bytes 147464 | tf_op jit(solution)/shard_map/ppermute | solution.py:17
  13.0 6.3 %collective-permute-start.1 = (bf16[3,64,128]{2,0,1:T(4,128)(2,1)S(1)}, bf16[3,64,128]{2,0,1:T(4,128)(2,1)S(1)}, u32[]{:S(2)}, u32[]{:S(2)}) collective-permute-start(bf16[3,64,128]{2,0,1:T(4,128)(2,1)S(1)} %get-tuple-element.102), channel_id=1, source_target_pairs={{8,0},{16,8},{24,16},{32,24},{40,32},{48,40},{56,48},{64,56},{72,6... | collective-permute-start | bytes 147464 | tf_op jit(solution)/shard_map/ppermute | solution.py:19
  19.1 9.9 %copy-start.12 = (f32[128]{0:T(128)S(1)}, f32[128]{0:T(128)}, u32[]{:S(2)}) copy-start(f32[128]{0:T(128)} %param.14) | copy-start | bytes 1540
  19.3 4.3 collective-permute-start.2
  21.9 4.1 collective-permute-start.3
  62.1 2.8 copy-start.8
  62.1 2.8 copy-start.9
  62.1 2.8 copy-start.10
  64.9 8.7 %copy-start.5 = (bf16[128,64,128]{2,1,0:T(8,128)(2,1)S(1)}, bf16[128,64,128]{2,1,0:T(8,128)(2,1)}, u32[]{:S(2)}) copy-start(bf16[128,64,128]{2,1,0:T(8,128)(2,1)} %param.12) | copy-start | bytes 6291460
  64.9 8.7 %copy-start.13 = (bf16[512,128]{1,0:T(8,128)(2,1)S(1)}, bf16[512,128]{1,0:T(8,128)(2,1)}, u32[]{:S(2)}) copy-start(bf16[512,128]{1,0:T(8,128)(2,1)} %param.19) | copy-start | bytes 393220
  93.4 32.8 %slice-start = ((s8[8388608]{0:T(1024)(128)(4,1)}), s8[4194304]{0:T(1024)(128)(4,1)S(1)}, s32[]{:S(2)}) async-start(s8[8388608]{0:T(1024)(128)(4,1)} %bitcast.185), calls=%async_computation.2 | async-start | bytes 8388608
  106.8 19.3 %copy-start.2 = (f32[128,64,128]{2,0,1:T(8,128)}, f32[128,64,128]{2,0,1:T(8,128)S(1)}, u32[]{:S(2)}) copy-start(f32[128,64,128]{2,0,1:T(8,128)S(1)} %get-tuple-element.92) | copy-start | bytes 12582916
  106.8 19.4 %slice-start.1 = ((s8[8388608]{0:T(1024)(128)(4,1)}), s8[4194304]{0:T(1024)(128)(4,1)S(1)}, s32[]{:S(2)}) async-start(s8[8388608]{0:T(1024)(128)(4,1)} %bitcast.185), calls=%async_computation.3 | async-start | bytes 8388608
  117.9 8.3 %copy-start.6 = (bf16[128,64,128]{2,1,0:T(8,128)(2,1)S(1)}, bf16[128,64,128]{2,1,0:T(8,128)(2,1)}, u32[]{:S(2)}) copy-start(bf16[128,64,128]{2,1,0:T(8,128)(2,1)} %param.12) | copy-start | bytes 6291460
  126.2 4.4 copy-start.14
  235.9 7.1 %collective-permute-start.4 = (f32[3,64,128]{2,0,1:T(4,128)S(1)}, f32[3,64,128]{2,0,1:T(4,128)S(1)}, u32[]{:S(2)}, u32[]{:S(2)}) collective-permute-start(f32[3,64,128]{2,0,1:T(4,128)S(1)} %get-tuple-element.97), channel_id=1, source_target_pairs={{0,8},{8,16},{16,24},{24,32},{32,40},{40,48},{48,56},{56,64},{64,7... | collective-permute-start | bytes 294920 | tf_op jit(solution)/shard_map/ppermute | solution.py:17
  235.9 7.1 %collective-permute-start.5 = (f32[3,64,128]{2,0,1:T(4,128)S(1)}, f32[3,64,128]{2,0,1:T(4,128)S(1)}, u32[]{:S(2)}, u32[]{:S(2)}) collective-permute-start(f32[3,64,128]{2,0,1:T(4,128)S(1)} %get-tuple-element.98), channel_id=1, source_target_pairs={{8,0},{16,8},{24,16},{32,24},{40,32},{48,40},{56,48},{64,56},{72,6... | collective-permute-start | bytes 294920 | tf_op jit(solution)/shard_map/ppermute | solution.py:19
  241.2 197.0 %all-reduce.9.cloned.1.call-start = ((), (), s32[]{:S(2)}) async-start(), calls=%async_computation.1 | async-start | bytes 1048576 | tf_op jit(solution)/shard_map/psum | solution.py:142
  241.3 10.5 %copy-start.3 = (f32[128,64,128]{2,0,1:T(8,128)S(1)}, f32[128,64,128]{2,0,1:T(8,128)}, u32[]{:S(2)}) copy-start(f32[128,64,128]{2,0,1:T(8,128)} %copy-done.2) | copy-start | bytes 12582916
  244.1 5.5 %collective-permute-start.6 = (f32[134,3,128]{2,0,1:T(8,128)S(1)}, f32[134,3,128]{2,0,1:T(8,128)S(1)}, u32[]{:S(2)}, u32[]{:S(2)}) collective-permute-start(f32[134,3,128]{2,0,1:T(8,128)S(1)} %get-tuple-element.95), channel_id=1, source_target_pairs={{0,1},{1,2},{2,3},{3,4},{4,5},{5,6},{6,7},{7,0},{8,9},{9,10},{10,1... | collective-permute-start | bytes 617480 | tf_op jit(solution)/shard_map/ppermute | solution.py:17
  246.5 5.2 %collective-permute-start.7 = (f32[134,3,128]{2,0,1:T(8,128)S(1)}, f32[134,3,128]{2,0,1:T(8,128)S(1)}, u32[]{:S(2)}, u32[]{:S(2)}) collective-permute-start(f32[134,3,128]{2,0,1:T(8,128)S(1)} %get-tuple-element.96), channel_id=1, source_target_pairs={{1,0},{2,1},{3,2},{4,3},{5,4},{6,5},{7,6},{0,7},{9,8},{10,9},{11,1... | collective-permute-start | bytes 617480 | tf_op jit(solution)/shard_map/ppermute | solution.py:19
  322.3 119.3 %copy-start.1 = (bf16[128,512]{1,0:T(8,128)(2,1)S(1)}, bf16[128,512]{1,0:T(8,128)(2,1)}, u32[]{:S(2)}) copy-start(bf16[128,512]{1,0:T(8,128)(2,1)} %param.17) | copy-start | bytes 393220
Sparse Core Ops, SparseCore 0:
  241.3 80.8 all-reduce.6
  324.6 59.6 all-reduce.8
